TPU v7x, 512 devices: a whole 4x8x8 slice. The times are simulated.
512 devices in a mesh: gy: 32 (over z, x), gx: 16 (over y, core).
Axes of the slice: x: 4, y: 8, z: 8, core: 2. Of those that a mesh axis runs over, the one named last changes fastest.
Arguments:
- ensemble: float32 [64, 256, 2048], P(None, 'gy', 'gx'), may hold values from -6 to 6
- flow: float32 [3, 256, 2048], P(None, 'gy', 'gx')
- obs_cell: int32 [32, 16, 4], P('gy', 'gx'), may hold values from 0 to 1023
- obs_value: float32 [32, 16, 4], P('gy', 'gx'), may hold values from -6 to 6
- obs_var: float32 [32, 16, 4], P('gy', 'gx'), may hold values from 4 to 16
Outputs:
- analysis: float32 [64, 256, 2048], P(None, 'gy', 'gx')
All inputs are finite; a program needn't handle non-finite values.
Results may differ from a plain program's by a relative error of at most 0.0001.
Values sent between devices are 32-bit elements; how exact they have to be, the bound alone decides.
A program may use at most 64 MiB of HBM per device.

v0:
```python
import jax
import jax.numpy as jnp
from jax import lax
from jax.sharding import PartitionSpec as P


def extended(block, sides, width):
    for axis, dim in sides:
        count = lax.axis_size(axis)
        forward = [(i, i + 1) for i in range(count - 1)]
        backward = [(target, source) for source, target in forward]
        low = lax.ppermute(
            lax.slice_in_dim(block, block.shape[dim] - width, None, axis=dim), axis, forward
        )
        high = lax.ppermute(lax.slice_in_dim(block, 0, width, axis=dim), axis, backward)
        block = jnp.concatenate([low, block, high], axis=dim)
    return block


def advance(padded, coeffs):
    state_grid = padded[:, 1:-1, 1:-1]
    north = padded[:, :-2, 1:-1]
    south = padded[:, 2:, 1:-1]
    west = padded[:, 1:-1, :-2]
    east = padded[:, 1:-1, 2:]
    spread = coeffs[0] * (north + south + west + east - 4.0 * state_grid)
    return state_grid + spread - 0.5 * coeffs[1] * (east - west) - 0.5 * coeffs[2] * (south - north)


def border_update(state_grid, flow):
    padded = extended(state_grid, (("gy", 1), ("gx", 2)), 1)
    return advance(padded, flow)


def tri_solve(matrix, rhs):
    return lax.linalg.triangular_solve(matrix, rhs, left_side=True, lower=True, transpose_a=True)


def body(ensemble, flow, obs_cell, obs_value, obs_var):
    members = ensemble.shape[0]
    predicted_state = border_update(border_update(ensemble, flow), flow)
    ensemble_average = jnp.mean(predicted_state, axis=0)
    member_deviation = predicted_state - ensemble_average
    flat_anomaly = member_deviation.reshape(members, -1)
    cells = obs_cell.reshape(-1)
    factor = lax.rsqrt(obs_var.reshape(-1))
    scaled = jnp.take(flat_anomaly, cells, axis=1) * factor
    innovation = (obs_value.reshape(-1) - jnp.take(ensemble_average.reshape(-1), cells)) * factor
    eye = jnp.eye(members, dtype=jnp.float32)
    local_gram = jnp.dot(scaled, scaled.T, precision=lax.Precision.HIGHEST)
    local_target = jnp.dot(scaled, innovation, precision=lax.Precision.HIGHEST)
    gram, target = lax.psum((local_gram, local_target), ("gy", "gx"))
    lower = jnp.linalg.cholesky(gram + (members - 1.0) * eye)
    inverse = tri_solve(lower, eye)
    weights = jnp.dot(
        inverse,
        jnp.dot(inverse.T, target, precision=lax.Precision.HIGHEST),
        precision=lax.Precision.HIGHEST,
    )
    transform = jnp.sqrt(members - 1.0) * inverse + weights[:, None]
    update = jnp.dot(transform.T, flat_anomaly, precision=lax.Precision.HIGHEST)
    return ensemble_average + update.reshape(member_deviation.shape)


def solution(mesh):
    return jax.shard_map(
        body,
        mesh=mesh,
        in_specs=(
            P(None, "gy", "gx"),
            P(None, "gy", "gx"),
            P("gy", "gx", None),
            P("gy", "gx", None),
            P("gy", "gx", None),
        ),
        out_specs=P(None, "gy", "gx"),
        check_vma=False,
    )
```

profile of v0, /device:TPU:1, one launch (start us, length us, event | category | flops | bytes accessed | tf_op | source)
XLA Modules:
  0.0 169.7 jit_solution(2727058517683121358)
XLA Ops:
  0.0 1.1 copy.23
  1.1 3.9 %collective-permute-start = (f32[64,1,128]{2,0,1:T(8,128)S(1)}, f32[64,1,128]{2,0,1:T(8,128)S(1)}, u32[]{:S(2)}, u32[]{:S(2)}) collective-permute-start(f32[64,1,128]{2,0,1:T(8,128)S(1)} %get-tuple-element.18), channel_id=1, source_target_pairs={{0,16},{16,32},{32,48},{48,64},{64,80},{80,96},{96,112},{112,128},... | collective-permute-start | bytes 98312 | tf_op jit(solution)/shard_map/ppermute | solution.py:12
  5.1 1.3 collective-permute-start.1
  6.5 3.2 %collective-permute-done.1 = f32[64,1,128]{2,0,1:T(8,128)S(1)} collective-permute-done((f32[64,1,128]{2,0,1:T(8,128)S(1)}, f32[64,1,128]{2,0,1:T(8,128)S(1)}, u32[]{:S(2)}, u32[]{:S(2)}) %collective-permute-start.1) | collective-permute-done | bytes 32800 | tf_op jit(solution)/shard_map/ppermute | solution.py:15
  9.9 5.2 %collective-permute-start.2 = (f32[64,10,1]{2,0,1:T(8,128)S(1)}, f32[64,10,1]{2,0,1:T(8,128)S(1)}, u32[]{:S(2)}, u32[]{:S(2)}) collective-permute-start(f32[64,10,1]{2,0,1:T(8,128)S(1)} %get-tuple-element.11), channel_id=1, source_target_pairs={{0,1},{1,2},{2,3},{3,4},{4,5},{5,6},{6,7},{7,8},{8,9},{9,10},{10,1... | collective-permute-start | bytes 7688 | tf_op jit(solution)/shard_map/ppermute | solution.py:12
  15.1 3.4 %collective-permute-start.3 = (f32[64,10,1]{2,0,1:T(8,128)S(1)}, f32[64,10,1]{2,0,1:T(8,128)S(1)}, u32[]{:S(2)}, u32[]{:S(2)}) collective-permute-start(f32[64,10,1]{2,0,1:T(8,128)S(1)} %get-tuple-element.12), channel_id=1, source_target_pairs={{1,0},{2,1},{3,2},{4,3},{5,4},{6,5},{7,6},{8,7},{9,8},{10,9},{11,1... | collective-permute-start | bytes 7688 | tf_op jit(solution)/shard_map/ppermute | solution.py:15
  18.5 0.6 collective-permute-done.2
  19.1 4.4 %collective-permute-done.3 = f32[64,10,1]{2,0,1:T(8,128)S(1)} collective-permute-done((f32[64,10,1]{2,0,1:T(8,128)S(1)}, f32[64,10,1]{2,0,1:T(8,128)S(1)}, u32[]{:S(2)}, u32[]{:S(2)}) %collective-permute-start.3) | collective-permute-done | bytes 2592 | tf_op jit(solution)/shard_map/ppermute | solution.py:15
  23.8 3.1 %collective-permute-start.4 = (f32[64,1,128]{2,0,1:T(8,128)S(1)}, f32[64,1,128]{2,0,1:T(8,128)S(1)}, u32[]{:S(2)}, u32[]{:S(2)}) collective-permute-start(f32[64,1,128]{2,0,1:T(8,128)S(1)} %get-tuple-element.15), channel_id=1, source_target_pairs={{0,16},{16,32},{32,48},{48,64},{64,80},{80,96},{96,112},{112,128},... | collective-permute-start | bytes 98312 | tf_op jit(solution)/shard_map/ppermute | solution.py:12
  26.9 1.3 collective-permute-start.5
  28.3 3.3 %collective-permute-done.5 = f32[64,1,128]{2,0,1:T(8,128)S(1)} collective-permute-done((f32[64,1,128]{2,0,1:T(8,128)S(1)}, f32[64,1,128]{2,0,1:T(8,128)S(1)}, u32[]{:S(2)}, u32[]{:S(2)}) %collective-permute-start.5) | collective-permute-done | bytes 32800 | tf_op jit(solution)/shard_map/ppermute | solution.py:15
  31.8 3.2 %collective-permute-start.6 = (f32[64,10,1]{2,0,1:T(8,128)S(1)}, f32[64,10,1]{2,0,1:T(8,128)S(1)}, u32[]{:S(2)}, u32[]{:S(2)}) collective-permute-start(f32[64,10,1]{2,0,1:T(8,128)S(1)} %get-tuple-element.9), channel_id=1, source_target_pairs={{0,1},{1,2},{2,3},{3,4},{4,5},{5,6},{6,7},{7,8},{8,9},{9,10},{10,1... | collective-permute-start | bytes 7688 | tf_op jit(solution)/shard_map/ppermute | solution.py:12
  35.0 1.9 %collective-permute-start.7 = (f32[64,10,1]{2,0,1:T(8,128)S(1)}, f32[64,10,1]{2,0,1:T(8,128)S(1)}, u32[]{:S(2)}, u32[]{:S(2)}) collective-permute-start(f32[64,10,1]{2,0,1:T(8,128)S(1)} %get-tuple-element.10), channel_id=1, source_target_pairs={{1,0},{2,1},{3,2},{4,3},{5,4},{6,5},{7,6},{8,7},{9,8},{10,9},{11,1... | collective-permute-start | bytes 7688 | tf_op jit(solution)/shard_map/ppermute | solution.py:15
  36.9 2.1 %collective-permute-done.6 = f32[64,10,1]{2,0,1:T(8,128)S(1)} collective-permute-done((f32[64,10,1]{2,0,1:T(8,128)S(1)}, f32[64,10,1]{2,0,1:T(8,128)S(1)}, u32[]{:S(2)}, u32[]{:S(2)}) %collective-permute-start.6) | collective-permute-done | bytes 2592 | tf_op jit(solution)/shard_map/ppermute | solution.py:12
  39.0 4.4 %collective-permute-done.7 = f32[64,10,1]{2,0,1:T(8,128)S(1)} collective-permute-done((f32[64,10,1]{2,0,1:T(8,128)S(1)}, f32[64,10,1]{2,0,1:T(8,128)S(1)}, u32[]{:S(2)}, u32[]{:S(2)}) %collective-permute-start.7) | collective-permute-done | bytes 2592 | tf_op jit(solution)/shard_map/ppermute | solution.py:15
  43.9 0.6 gather_fusion
  44.5 0.6 gather_fusion.1
  46.0 109.7 %all-reduce = (f32[64,64]{1,0:T(8,128)S(1)}, f32[64]{0:T(128)S(1)}) all-reduce(f32[64,64]{1,0:T(8,128)S(1)} %fusion.13, f32[64]{0:T(128)S(1)} %convolution_bitcast_fusion.2), channel_id=1, replica_groups=mesh['gy'=32,'gx'=16] {'gy','gx'}, use_global_device_ids=true, to_apply=%region_1.2 | all-reduce | flops 4160 | bytes 33280 | tf_op jit(solution)/shard_map/psum | solution.py:52
  155.8 5.8 %cholesky.17 = f32[64,64]{1,0:T(8,128)S(1)} custom-call(f32[64,64]{1,0:T(8,128)S(1)} %fusion.7), custom_call_target="Cholesky" | custom-call | tf_op jit(solution)/shard_map/jit(cholesky)/cholesky | solution.py:53
  161.6 0.6 compare_reduce_fusion
  162.3 0.7 fusion.2
  162.9 4.9 %custom-call.6 = f32[1,64,64]{1,2,0:T(8,128)S(1)} custom-call(f32[1,64,64]{2,1,0:T(8,128)S(1)} %fusion.2), custom_call_target="InvertDiagBlocksLowerTriangular" | custom-call | tf_op jit(solution)/shard_map/triangular_solve | solution.py:36
  168.3 0.5 convolution_add_fusion
  168.8 0.9 copy.29
  (39 shorter events, 2.7 us)
Async XLA Ops:
  0.0 6.4 %copy-start = (f32[64,8,128]{2,1,0:T(8,128)S(1)}, f32[64,8,128]{2,1,0:T(8,128)}, u32[]{:S(2)}) copy-start(f32[64,8,128]{2,1,0:T(8,128)} %param.5) | copy-start | bytes 786436
  1.1 5.3 %copy-start.1 = (f32[3,8,128]{2,1,0:T(8,128)S(1)}, f32[3,8,128]{2,1,0:T(8,128)}, u32[]{:S(2)}) copy-start(f32[3,8,128]{2,1,0:T(8,128)} %param.6) | copy-start | bytes 36868
  1.1 5.3 %collective-permute-start = (f32[64,1,128]{2,0,1:T(8,128)S(1)}, f32[64,1,128]{2,0,1:T(8,128)S(1)}, u32[]{:S(2)}, u32[]{:S(2)}) collective-permute-start(f32[64,1,128]{2,0,1:T(8,128)S(1)} %get-tuple-element.18), channel_id=1, source_target_pairs={{0,16},{16,32},{32,48},{48,64},{64,80},{80,96},{96,112},{112,128},... | collective-permute-start | bytes 98312 | tf_op jit(solution)/shard_map/ppermute | solution.py:12
  5.1 1.3 copy-start.2
  5.1 4.7 %collective-permute-start.1 = (f32[64,1,128]{2,0,1:T(8,128)S(1)}, f32[64,1,128]{2,0,1:T(8,128)S(1)}, u32[]{:S(2)}, u32[]{:S(2)}) collective-permute-start(f32[64,1,128]{2,0,1:T(8,128)S(1)} %get-tuple-element.17), channel_id=1, source_target_pairs={{16,0},{32,16},{48,32},{64,48},{80,64},{96,80},{112,96},{128,112},... | collective-permute-start | bytes 98312 | tf_op jit(solution)/shard_map/ppermute | solution.py:15
  9.9 9.2 %collective-permute-start.2 = (f32[64,10,1]{2,0,1:T(8,128)S(1)}, f32[64,10,1]{2,0,1:T(8,128)S(1)}, u32[]{:S(2)}, u32[]{:S(2)}) collective-permute-start(f32[64,10,1]{2,0,1:T(8,128)S(1)} %get-tuple-element.11), channel_id=1, source_target_pairs={{0,1},{1,2},{2,3},{3,4},{4,5},{5,6},{6,7},{7,8},{8,9},{9,10},{10,1... | collective-permute-start | bytes 7688 | tf_op jit(solution)/shard_map/ppermute | solution.py:12
  15.1 8.4 %collective-permute-start.3 = (f32[64,10,1]{2,0,1:T(8,128)S(1)}, f32[64,10,1]{2,0,1:T(8,128)S(1)}, u32[]{:S(2)}, u32[]{:S(2)}) collective-permute-start(f32[64,10,1]{2,0,1:T(8,128)S(1)} %get-tuple-element.12), channel_id=1, source_target_pairs={{1,0},{2,1},{3,2},{4,3},{5,4},{6,5},{7,6},{8,7},{9,8},{10,9},{11,1... | collective-permute-start | bytes 7688 | tf_op jit(solution)/shard_map/ppermute | solution.py:15
  23.8 4.4 %copy-start.3 = (f32[1,1,4]{2,1,0:T(1,128)S(1)}, f32[1,1,4]{2,1,0:T(1,128)}, u32[]{:S(2)}) copy-start(f32[1,1,4]{2,1,0:T(1,128)} %param.9) | copy-start | bytes 52
  23.8 4.5 %collective-permute-start.4 = (f32[64,1,128]{2,0,1:T(8,128)S(1)}, f32[64,1,128]{2,0,1:T(8,128)S(1)}, u32[]{:S(2)}, u32[]{:S(2)}) collective-permute-start(f32[64,1,128]{2,0,1:T(8,128)S(1)} %get-tuple-element.15), channel_id=1, source_target_pairs={{0,16},{16,32},{32,48},{48,64},{64,80},{80,96},{96,112},{112,128},... | collective-permute-start | bytes 98312 | tf_op jit(solution)/shard_map/ppermute | solution.py:12
  26.9 4.7 %collective-permute-start.5 = (f32[64,1,128]{2,0,1:T(8,128)S(1)}, f32[64,1,128]{2,0,1:T(8,128)S(1)}, u32[]{:S(2)}, u32[]{:S(2)}) collective-permute-start(f32[64,1,128]{2,0,1:T(8,128)S(1)} %get-tuple-element.16), channel_id=1, source_target_pairs={{16,0},{32,16},{48,32},{64,48},{80,64},{96,80},{112,96},{128,112},... | collective-permute-start | bytes 98312 | tf_op jit(solution)/shard_map/ppermute | solution.py:15
  31.8 7.2 %collective-permute-start.6 = (f32[64,10,1]{2,0,1:T(8,128)S(1)}, f32[64,10,1]{2,0,1:T(8,128)S(1)}, u32[]{:S(2)}, u32[]{:S(2)}) collective-permute-start(f32[64,10,1]{2,0,1:T(8,128)S(1)} %get-tuple-element.9), channel_id=1, source_target_pairs={{0,1},{1,2},{2,3},{3,4},{4,5},{5,6},{6,7},{7,8},{8,9},{9,10},{10,1... | collective-permute-start | bytes 7688 | tf_op jit(solution)/shard_map/ppermute | solution.py:12
  35.0 8.4 %collective-permute-start.7 = (f32[64,10,1]{2,0,1:T(8,128)S(1)}, f32[64,10,1]{2,0,1:T(8,128)S(1)}, u32[]{:S(2)}, u32[]{:S(2)}) collective-permute-start(f32[64,10,1]{2,0,1:T(8,128)S(1)} %get-tuple-element.10), channel_id=1, source_target_pairs={{1,0},{2,1},{3,2},{4,3},{5,4},{6,5},{7,6},{8,7},{9,8},{10,9},{11,1... | collective-permute-start | bytes 7688 | tf_op jit(solution)/shard_map/ppermute | solution.py:15
  45.1 0.7 copy-start.4
where the time goes:
time: 170 us
  blocking collectives  110 us (65%)
  starting transfers between devices  23.3 us (14%)
  waiting for transfers between devices  18 us (11%)
  other arithmetic  12.8 us (8%)
  local copies, waits for them, and re-layouts  4.15 us (2%)
    psum x1, blocking collectives, body(): gram, target = lax.psum((local_gram, local_target), ('gy', 'gx'))  110 us
    ppermute x4, starting transfers between devices, extended(): lax.ppermute(lax.slice_in_dim(block, block.shape[dim] - width, None, axis...  15.4 us
    ppermute x4, waiting for transfers between devices, extended(): lax.ppermute(lax.slice_in_dim(block, 0, width, axis=dim), axis, backward)  15.3 us
    ppermute x4, starting transfers between devices, extended(): lax.ppermute(lax.slice_in_dim(block, 0, width, axis=dim), axis, backward)  7.9 us
    another operation x3, other arithmetic, body(): lower = jnp.linalg.cholesky(gram + (members - 1.0) * eye)  6.52 us
    another operation x2, other arithmetic, tri_solve(): lax.linalg.triangular_solve(matrix, rhs, left_side=True, lower=True, tran...  5.55 us
  transfers between devices with their start and end apart: 8, of which 6 were waited for; matrix products, arithmetic and copies ran while one was open for 0% of the time, Pallas kernels for 0%

commit v1 on v0

--- a/solution.py
+++ b/solution.py
@@ -49,7 +49,7 @@
     eye = jnp.eye(members, dtype=jnp.float32)
     local_gram = jnp.dot(scaled, scaled.T, precision=lax.Precision.HIGHEST)
     local_target = jnp.dot(scaled, innovation, precision=lax.Precision.HIGHEST)
-    gram, target = lax.psum((local_gram, local_target), ("gy", "gx"))
+    gram, target = lax.psum(lax.psum((local_gram, local_target), "gy"), "gx")
     lower = jnp.linalg.cholesky(gram + (members - 1.0) * eye)
     inverse = tri_solve(lower, eye)
     weights = jnp.dot(

time: 170 us -> 252 us (1.48)
  the two profiles are of different devices: /device:TPU:1 before, /device:TPU:288 now
where the time goes in v1:
time: 252 us
  blocking collectives  189 us (75%)
  starting transfers between devices  32.2 us (13%)
  other arithmetic  12.8 us (5%)
  waiting for transfers between devices  12.1 us (5%)
  local copies, waits for them, and re-layouts  4.15 us (2%)
    psum x2, blocking collectives, body(): gram, target = lax.psum(lax.psum((local_gram, local_target), 'gy'), 'gx')  189 us
    ppermute x4, starting transfers between devices, extended(): lax.ppermute(lax.slice_in_dim(block, 0, width, axis=dim), axis, backward)  23 us
    ppermute x4, starting transfers between devices, extended(): lax.ppermute(lax.slice_in_dim(block, block.shape[dim] - width, None, axis...  9.16 us
    another operation x3, other arithmetic, body(): lower = jnp.linalg.cholesky(gram + (members - 1.0) * eye)  6.52 us
    ppermute x4, waiting for transfers between devices, extended(): lax.ppermute(lax.slice_in_dim(block, 0, width, axis=dim), axis, backward)  6.5 us
    ppermute x4, waiting for transfers between devices, extended(): lax.ppermute(lax.slice_in_dim(block, block.shape[dim] - width, None, axis...  5.61 us
    another operation x2, other arithmetic, tri_solve(): lax.linalg.triangular_solve(matrix, rhs, left_side=True, lower=True, tran...  5.55 us
  transfers between devices with their start and end apart: 8, of which 6 were waited for; matrix products, arithmetic and copies ran while one was open for 0% of the time, Pallas kernels for 0%

profile of v1, /device:TPU:288, one launch (start us, length us, event | category | flops | bytes accessed | tf_op | source)
XLA Modules:
  0.0 252.1 jit_solution(8879926966451773441)
XLA Ops:
  0.0 1.1 copy.23
  1.1 3.4 %collective-permute-start = (f32[64,1,128]{2,0,1:T(8,128)S(1)}, f32[64,1,128]{2,0,1:T(8,128)S(1)}, u32[]{:S(2)}, u32[]{:S(2)}) collective-permute-start(f32[64,1,128]{2,0,1:T(8,128)S(1)} %get-tuple-element.20), channel_id=1, source_target_pairs={{0,16},{16,32},{32,48},{48,64},{64,80},{80,96},{96,112},{112,128},... | collective-permute-start | bytes 98312 | tf_op jit(solution)/shard_map/ppermute | solution.py:12
  4.5 5.8 %collective-permute-start.1 = (f32[64,1,128]{2,0,1:T(8,128)S(1)}, f32[64,1,128]{2,0,1:T(8,128)S(1)}, u32[]{:S(2)}, u32[]{:S(2)}) collective-permute-start(f32[64,1,128]{2,0,1:T(8,128)S(1)} %get-tuple-element.19), channel_id=1, source_target_pairs={{16,0},{32,16},{48,32},{64,48},{80,64},{96,80},{112,96},{128,112},... | collective-permute-start | bytes 98312 | tf_op jit(solution)/shard_map/ppermute | solution.py:15
  10.4 1.4 collective-permute-done.1
  12.0 1.9 collective-permute-start.2
  14.0 4.9 %collective-permute-start.3 = (f32[64,10,1]{2,0,1:T(8,128)S(1)}, f32[64,10,1]{2,0,1:T(8,128)S(1)}, u32[]{:S(2)}, u32[]{:S(2)}) collective-permute-start(f32[64,10,1]{2,0,1:T(8,128)S(1)} %get-tuple-element.14), channel_id=1, source_target_pairs={{1,0},{2,1},{3,2},{4,3},{5,4},{6,5},{7,6},{8,7},{9,8},{10,9},{11,1... | collective-permute-start | bytes 7688 | tf_op jit(solution)/shard_map/ppermute | solution.py:15
  18.8 2.8 %collective-permute-done.2 = f32[64,10,1]{2,0,1:T(8,128)S(1)} collective-permute-done((f32[64,10,1]{2,0,1:T(8,128)S(1)}, f32[64,10,1]{2,0,1:T(8,128)S(1)}, u32[]{:S(2)}, u32[]{:S(2)}) %collective-permute-start.2) | collective-permute-done | bytes 2592 | tf_op jit(solution)/shard_map/ppermute | solution.py:12
  21.6 1.8 collective-permute-done.3
  23.7 1.9 collective-permute-start.4
  25.6 7.5 %collective-permute-start.5 = (f32[64,1,128]{2,0,1:T(8,128)S(1)}, f32[64,1,128]{2,0,1:T(8,128)S(1)}, u32[]{:S(2)}, u32[]{:S(2)}) collective-permute-start(f32[64,1,128]{2,0,1:T(8,128)S(1)} %get-tuple-element.18), channel_id=1, source_target_pairs={{16,0},{32,16},{48,32},{64,48},{80,64},{96,80},{112,96},{128,112},... | collective-permute-start | bytes 98312 | tf_op jit(solution)/shard_map/ppermute | solution.py:15
  33.2 1.5 collective-permute-done.5
  35.0 1.9 collective-permute-start.6
  36.9 4.9 %collective-permute-start.7 = (f32[64,10,1]{2,0,1:T(8,128)S(1)}, f32[64,10,1]{2,0,1:T(8,128)S(1)}, u32[]{:S(2)}, u32[]{:S(2)}) collective-permute-start(f32[64,10,1]{2,0,1:T(8,128)S(1)} %get-tuple-element.12), channel_id=1, source_target_pairs={{1,0},{2,1},{3,2},{4,3},{5,4},{6,5},{7,6},{8,7},{9,8},{10,9},{11,1... | collective-permute-start | bytes 7688 | tf_op jit(solution)/shard_map/ppermute | solution.py:15
  41.8 2.8 %collective-permute-done.6 = f32[64,10,1]{2,0,1:T(8,128)S(1)} collective-permute-done((f32[64,10,1]{2,0,1:T(8,128)S(1)}, f32[64,10,1]{2,0,1:T(8,128)S(1)}, u32[]{:S(2)}, u32[]{:S(2)}) %collective-permute-start.6) | collective-permute-done | bytes 2592 | tf_op jit(solution)/shard_map/ppermute | solution.py:12
  44.6 1.8 collective-permute-done.7
  46.9 0.6 gather_fusion
  47.4 0.6 gather_fusion.1
  48.9 143.3 %all-reduce = (f32[64,64]{1,0:T(8,128)S(1)}, f32[64]{0:T(128)S(1)}) all-reduce(f32[64,64]{1,0:T(8,128)S(1)} %fusion.13, f32[64]{0:T(128)S(1)} %convolution_bitcast_fusion.2), channel_id=1, replica_groups=mesh['gy'=32,'gx'=16] {'gy'}, use_global_device_ids=true, to_apply=%region_1.2 | all-reduce | flops 4160 | bytes 33280 | tf_op jit(solution)/shard_map/psum | solution.py:52
  192.3 45.8 %all-reduce.1 = (f32[64,64]{1,0:T(8,128)S(1)}, f32[64]{0:T(128)S(1)}) all-reduce(f32[64,64]{1,0:T(8,128)S(1)} %get-tuple-element.5, f32[64]{0:T(128)S(1)} %get-tuple-element.6), channel_id=1, replica_groups=mesh['gy'=32,'gx'=16] {'gx'}, use_global_device_ids=true, to_apply=%region_2.3 | all-reduce | flops 4160 | bytes 33280 | tf_op jit(solution)/shard_map/psum | solution.py:52
  238.2 5.8 %cholesky.17 = f32[64,64]{1,0:T(8,128)S(1)} custom-call(f32[64,64]{1,0:T(8,128)S(1)} %fusion.7), custom_call_target="Cholesky" | custom-call | tf_op jit(solution)/shard_map/jit(cholesky)/cholesky | solution.py:53
  244.0 0.6 compare_reduce_fusion
  244.7 0.7 fusion.2
  245.3 4.9 %custom-call.6 = f32[1,64,64]{1,2,0:T(8,128)S(1)} custom-call(f32[1,64,64]{2,1,0:T(8,128)S(1)} %fusion.2), custom_call_target="InvertDiagBlocksLowerTriangular" | custom-call | tf_op jit(solution)/shard_map/triangular_solve | solution.py:36
  251.2 0.9 copy.29
  (40 shorter events, 3.2 us)
Async XLA Ops:
  0.0 10.4 %copy-start = (f32[64,8,128]{2,1,0:T(8,128)S(1)}, f32[64,8,128]{2,1,0:T(8,128)}, u32[]{:S(2)}) copy-start(f32[64,8,128]{2,1,0:T(8,128)} %param.5) | copy-start | bytes 786436
  1.1 9.2 %copy-start.1 = (f32[3,8,128]{2,1,0:T(8,128)S(1)}, f32[3,8,128]{2,1,0:T(8,128)}, u32[]{:S(2)}) copy-start(f32[3,8,128]{2,1,0:T(8,128)} %param.6) | copy-start | bytes 36868
  1.1 9.2 %collective-permute-start = (f32[64,1,128]{2,0,1:T(8,128)S(1)}, f32[64,1,128]{2,0,1:T(8,128)S(1)}, u32[]{:S(2)}, u32[]{:S(2)}) collective-permute-start(f32[64,1,128]{2,0,1:T(8,128)S(1)} %get-tuple-element.20), channel_id=1, source_target_pairs={{0,16},{16,32},{32,48},{48,64},{64,80},{80,96},{96,112},{112,128},... | collective-permute-start | bytes 98312 | tf_op jit(solution)/shard_map/ppermute | solution.py:12
  4.5 5.8 %copy-start.2 = (s32[1,1,4]{2,1,0:T(1,128)S(1)}, s32[1,1,4]{2,1,0:T(1,128)}, u32[]{:S(2)}) copy-start(s32[1,1,4]{2,1,0:T(1,128)} %param.7) | copy-start | bytes 52
  4.5 7.3 %collective-permute-start.1 = (f32[64,1,128]{2,0,1:T(8,128)S(1)}, f32[64,1,128]{2,0,1:T(8,128)S(1)}, u32[]{:S(2)}, u32[]{:S(2)}) collective-permute-start(f32[64,1,128]{2,0,1:T(8,128)S(1)} %get-tuple-element.19), channel_id=1, source_target_pairs={{16,0},{32,16},{48,32},{64,48},{80,64},{96,80},{112,96},{128,112},... | collective-permute-start | bytes 98312 | tf_op jit(solution)/shard_map/ppermute | solution.py:15
  12.0 9.6 %collective-permute-start.2 = (f32[64,10,1]{2,0,1:T(8,128)S(1)}, f32[64,10,1]{2,0,1:T(8,128)S(1)}, u32[]{:S(2)}, u32[]{:S(2)}) collective-permute-start(f32[64,10,1]{2,0,1:T(8,128)S(1)} %get-tuple-element.13), channel_id=1, source_target_pairs={{0,1},{1,2},{2,3},{3,4},{4,5},{5,6},{6,7},{7,8},{8,9},{9,10},{10,1... | collective-permute-start | bytes 7688 | tf_op jit(solution)/shard_map/ppermute | solution.py:12
  14.0 9.4 %collective-permute-start.3 = (f32[64,10,1]{2,0,1:T(8,128)S(1)}, f32[64,10,1]{2,0,1:T(8,128)S(1)}, u32[]{:S(2)}, u32[]{:S(2)}) collective-permute-start(f32[64,10,1]{2,0,1:T(8,128)S(1)} %get-tuple-element.14), channel_id=1, source_target_pairs={{1,0},{2,1},{3,2},{4,3},{5,4},{6,5},{7,6},{8,7},{9,8},{10,9},{11,1... | collective-permute-start | bytes 7688 | tf_op jit(solution)/shard_map/ppermute | solution.py:15
  23.7 9.5 %copy-start.3 = (f32[1,1,4]{2,1,0:T(1,128)S(1)}, f32[1,1,4]{2,1,0:T(1,128)}, u32[]{:S(2)}) copy-start(f32[1,1,4]{2,1,0:T(1,128)} %param.9) | copy-start | bytes 52
  23.7 9.5 %collective-permute-start.4 = (f32[64,1,128]{2,0,1:T(8,128)S(1)}, f32[64,1,128]{2,0,1:T(8,128)S(1)}, u32[]{:S(2)}, u32[]{:S(2)}) collective-permute-start(f32[64,1,128]{2,0,1:T(8,128)S(1)} %get-tuple-element.17), channel_id=1, source_target_pairs={{0,16},{16,32},{32,48},{48,64},{64,80},{80,96},{96,112},{112,128},... | collective-permute-start | bytes 98312 | tf_op jit(solution)/shard_map/ppermute | solution.py:12
  25.6 9.1 %collective-permute-start.5 = (f32[64,1,128]{2,0,1:T(8,128)S(1)}, f32[64,1,128]{2,0,1:T(8,128)S(1)}, u32[]{:S(2)}, u32[]{:S(2)}) collective-permute-start(f32[64,1,128]{2,0,1:T(8,128)S(1)} %get-tuple-element.18), channel_id=1, source_target_pairs={{16,0},{32,16},{48,32},{64,48},{80,64},{96,80},{112,96},{128,112},... | collective-permute-start | bytes 98312 | tf_op jit(solution)/shard_map/ppermute | solution.py:15
  35.0 9.6 %collective-permute-start.6 = (f32[64,10,1]{2,0,1:T(8,128)S(1)}, f32[64,10,1]{2,0,1:T(8,128)S(1)}, u32[]{:S(2)}, u32[]{:S(2)}) collective-permute-start(f32[64,10,1]{2,0,1:T(8,128)S(1)} %get-tuple-element.11), channel_id=1, source_target_pairs={{0,1},{1,2},{2,3},{3,4},{4,5},{5,6},{6,7},{7,8},{8,9},{9,10},{10,1... | collective-permute-start | bytes 7688 | tf_op jit(solution)/shard_map/ppermute | solution.py:12
  36.9 9.4 %collective-permute-start.7 = (f32[64,10,1]{2,0,1:T(8,128)S(1)}, f32[64,10,1]{2,0,1:T(8,128)S(1)}, u32[]{:S(2)}, u32[]{:S(2)}) collective-permute-start(f32[64,10,1]{2,0,1:T(8,128)S(1)} %get-tuple-element.12), channel_id=1, source_target_pairs={{1,0},{2,1},{3,2},{4,3},{5,4},{6,5},{7,6},{8,7},{9,8},{10,9},{11,1... | collective-permute-start | bytes 7688 | tf_op jit(solution)/shard_map/ppermute | solution.py:15
  48.1 0.7 copy-start.4
